TPU v7x, 32 devices: a whole 2x2x4 slice. The times are simulated.
32 devices in a mesh: row: 4 (over z), col: 8 (over y, x, core).
Axes of the slice: x: 2, y: 2, z: 4, core: 2. Of those that a mesh axis runs over, the one named last changes fastest.
Arguments:
- tokens: bfloat16 [512, 8192], P('col', 'row'), may hold values from -6 to 6
- w_gate: bfloat16 [8192, 16384], P('row', 'col'), may hold values from -0.09375 to 0.09375
- w_up: bfloat16 [8192, 16384], P('row', 'col'), may hold values from -0.09375 to 0.09375
- w_down: bfloat16 [16384, 8192], P('col', 'row'), may hold values from -0.0625 to 0.0625
- mask_in: int32 [64, 32], P('col', 'row'), may hold values 0 or 1
- mask_out: int32 [64, 32], P('col', 'row'), may hold values 0 or 1
- out_grad: bfloat16 [512, 8192], P('col', 'row'), may hold values from -6 to 6
Outputs:
- output: bfloat16 [512, 8192], P('col', 'row')
- tokens_grad: bfloat16 [512, 8192], P('col', 'row')
- gate_wgrad: bfloat16 [8192, 16384], P('row', 'col')
- up_wgrad: bfloat16 [8192, 16384], P('row', 'col')
- down_wgrad: bfloat16 [16384, 8192], P('col', 'row')
All inputs are finite; a program needn't handle non-finite values. No bound on the sum of `mask_in` or of `mask_out` on one device may be relied on, other than what follows from the above.
Results may differ from a plain program's by a relative error of at most 0.0049.
Values may be sent and summed in bfloat16 or wider, within the bound.
A program may use at most 128 MiB of HBM per device.

v0:
```python
import jax
import jax.numpy as jnp
from jax import lax
from jax.sharding import PartitionSpec as P

BLOCK = 256


def spread(mask_tile):
    return jnp.repeat(jnp.repeat(mask_tile.T, BLOCK, axis=0), BLOCK, axis=1)


def transposed_right(left, right):
    return lax.dot_general(
        left, right, (((1,), (1,)), ((), ())), preferred_element_type=jnp.float32
    )


def transposed_left(left, right):
    return lax.dot_general(
        left, right, (((0,), (0,)), ((), ())), preferred_element_type=jnp.float32
    )


def local(tokens, w_gate, w_up, w_down, mask_in, mask_out, out_grad):
    keep_in = spread(mask_in).astype(jnp.bfloat16)
    keep_out = spread(mask_out).T.astype(jnp.bfloat16)
    gate_masked = w_gate * keep_in
    up_masked = w_up * keep_in
    down_masked = w_down * keep_out
    hidden_width = w_gate.shape[1]
    x_panel = lax.all_gather(tokens, "col", axis=0, tiled=True)
    row_block = x_panel
    gate_part = jnp.dot(row_block, gate_masked, preferred_element_type=jnp.float32)
    up_part = jnp.dot(row_block, up_masked, preferred_element_type=jnp.float32)
    joined = lax.psum_scatter(
        jnp.concatenate([gate_part, up_part], axis=1), "row", scatter_dimension=0, tiled=True
    )
    gate = joined[:, :hidden_width]
    up = joined[:, hidden_width:]
    sigmoid_gate = jax.nn.sigmoid(gate)
    hidden_share = (gate * sigmoid_gate * up).astype(jnp.bfloat16)
    hidden_full = lax.all_gather(hidden_share, "row", axis=0, tiled=True)
    row_block = hidden_full
    output = lax.psum_scatter(
        jnp.dot(row_block, down_masked, preferred_element_type=jnp.float32),
        "col",
        scatter_dimension=0,
        tiled=True,
    ).astype(jnp.bfloat16)
    dy_panel = lax.all_gather(out_grad, "col", axis=0, tiled=True)
    down_wgrad = (transposed_left(hidden_full, dy_panel) * keep_out.astype(jnp.float32)).astype(
        jnp.bfloat16
    )
    row_block = dy_panel
    hidden_grad = lax.psum_scatter(
        transposed_right(row_block, down_masked), "row", scatter_dimension=0, tiled=True
    )
    up_grad = (hidden_grad * gate * sigmoid_gate).astype(jnp.bfloat16)
    gate_grad = (hidden_grad * up * sigmoid_gate * (1.0 + gate * (1.0 - sigmoid_gate))).astype(
        jnp.bfloat16
    )
    gate_full, up_full = (
        lax.all_gather(gate_grad, "row", axis=0, tiled=True),
        lax.all_gather(up_grad, "row", axis=0, tiled=True),
    )
    keep_wide = keep_in.astype(jnp.float32)
    gate_wgrad = (transposed_left(x_panel, gate_full) * keep_wide).astype(jnp.bfloat16)
    up_wgrad = (transposed_left(x_panel, up_full) * keep_wide).astype(jnp.bfloat16)
    tokens_grad = lax.psum_scatter(
        transposed_right(gate_full, gate_masked) + transposed_right(up_full, up_masked),
        "col",
        scatter_dimension=0,
        tiled=True,
    ).astype(jnp.bfloat16)
    return (output, tokens_grad, gate_wgrad, up_wgrad, down_wgrad)


def solution(mesh):
    placed = (
        P("col", "row"),
        P("row", "col"),
        P("row", "col"),
        P("col", "row"),
        P("col", "row"),
        P("col", "row"),
        P("col", "row"),
    )
    return jax.shard_map(
        local,
        mesh=mesh,
        in_specs=placed,
        out_specs=(
            P("col", "row"),
            P("col", "row"),
            P("row", "col"),
            P("row", "col"),
            P("col", "row"),
        ),
        check_vma=False,
    )
```

profile of v0, /device:TPU:27, one launch (start us, length us, event | category | flops | bytes accessed | tf_op | source)
XLA Modules:
  0.0 552.7 jit_solution(6437327898248120053)
XLA Ops:
  9.6 7.3 %bitcast_multiply_fusion.2 = bf16[2048,2048]{1,0:T(8,128)(2,1)} fusion(bf16[2048,2048]{1,0:T(8,128)(2,1)} %param.10, bf16[2048,8]{0,1:T(8,128)(2,1)S(1)} %bitcast.48), kind=kLoop, calls=%fused_computation.7 | loop fusion | flops 4194304 | bytes 16809984 | tf_op jit(solution)/shard_map/mul | solution.py:30
  16.9 22.1 %all-gather.10.cloned.1.call-done = bf16[512,2048]{1,0:T(8,128)(2,1)} async-done(((bf16[64,2048]{1,0:T(8,128)(2,1)}), bf16[512,2048]{1,0:T(8,128)(2,1)}) %all-gather.10.cloned.1.call-update) | async-done | bytes 2097168 | tf_op jit(solution)/shard_map/all_gather | solution.py:51
  39.0 10.5 %convolution_bitcast_fusion = f32[512,2048]{0,1:T(8,128)} fusion(bf16[2048,2048]{1,0:T(8,128)(2,1)} %bitcast_multiply_fusion.2, bf16[512,2048]{1,0:T(8,128)(2,1)} %all-gather.10.cloned.1.call-done), kind=kOutput, calls=%fused_computation.9 | convolution fusion | flops 4294967296 | bytes 14680064 | tf_op jit(solution)/shard_map/dot_general | solution.py:14
  50.3 12.2 %copy.13 = bf16[2048,2048]{0,1:T(8,128)(2,1)} copy(bf16[2048,2048]{1,0:T(8,128)(2,1)} %param.8) | data formatting | bytes 16777216 | tf_op args[1]
  62.6 12.3 %copy.14 = bf16[2048,2048]{0,1:T(8,128)(2,1)} copy(bf16[2048,2048]{1,0:T(8,128)(2,1)} %param.9) | data formatting | bytes 16777216 | tf_op args[2]
  74.9 13.5 %bitcast_multiply_fusion.1 = (bf16[2048,2048]{0,1:T(8,128)(2,1)}, bf16[2048,2048]{0,1:T(8,128)(2,1)}) fusion(bf16[2048,2048]{0,1:T(8,128)(2,1)} %copy.13, bf16[2048,8]{0,1:T(8,128)(2,1)S(1)} %bitcast.50, bf16[2048,2048]{0,1:T(8,128)(2,1)} %copy.14), kind=kLoop, calls=%fused_computation.3 | loop fusion | flops 8388608 | bytes 33587200 | tf_op jit(solution)/shard_map/mul | solution.py:28
  88.4 7.9 %convolution_bitcast_fusion.1 = f32[512,2048]{0,1:T(8,128)S(1)} fusion(bf16[2048,2048]{0,1:T(8,128)(2,1)} %get-tuple-element.14, bf16[512,2048]{1,0:T(8,128)(2,1)} %all-gather.6.cloned.1.call-done), kind=kOutput, calls=%fused_computation.10 | convolution fusion | flops 4294967296 | bytes 14680064 | tf_op jit(solution)/shard_map/dot_general | solution.py:35
  96.3 4.8 convolution_bitcast_fusion.2
  101.1 4.2 pad_maximum_fusion
  105.4 41.5 %reduce-scatter.9.cloned.1.call-done = f32[128,2048]{0,1:T(8,128)} async-done(((f32[512,2048]{0,1:T(8,128)}), f32[128,2048]{0,1:T(8,128)}) %reduce-scatter.9.cloned.1.call-update) | async-done | bytes 1048592 | tf_op jit(solution)/shard_map/reduce_scatter | solution.py:56
  146.9 147.4 %reduce-scatter.5.cloned.1.call-done = f32[128,4096]{0,1:T(8,128)} async-done(((f32[512,4096]{0,1:T(8,128)}), f32[128,4096]{0,1:T(8,128)}) %reduce-scatter.5.cloned.1.call-update) | async-done | bytes 2097168 | tf_op jit(solution)/shard_map/reduce_scatter | solution.py:36
  294.3 3.5 multiply_convert_fusion.1
  299.5 43.1 %all-gather.12.cloned.1.call-done = bf16[512,2048]{0,1:T(8,128)(2,1)} async-done(((bf16[128,2048]{0,1:T(8,128)(2,1)}), bf16[512,2048]{0,1:T(8,128)(2,1)}) %all-gather.12.cloned.1.call-update) | async-done | bytes 2097168 | tf_op jit(solution)/shard_map/all_gather | solution.py:64
  342.6 10.6 %fusion.3 = f32[512,2048]{1,0:T(8,128)} fusion(bf16[512,2048]{0,1:T(8,128)(2,1)} %all-gather.12.cloned.1.call-done, bf16[2048,2048]{0,1:T(8,128)(2,1)} %get-tuple-element.13), kind=kOutput, calls=%fused_computation.20 | convolution fusion | flops 4294967296 | bytes 14680064 | tf_op jit(solution)/shard_map/dot_general | solution.py:14
  353.2 35.3 %all-gather.14.cloned.1.call-done = bf16[512,2048]{0,1:T(8,128)(2,1)} async-done(((bf16[128,2048]{0,1:T(8,128)(2,1)}), bf16[512,2048]{0,1:T(8,128)(2,1)}) %all-gather.14.cloned.1.call-update) | async-done | bytes 2097168 | tf_op jit(solution)/shard_map/all_gather | solution.py:65
  388.5 11.7 %convolution_add_fusion = f32[512,2048]{1,0:T(8,128)} fusion(f32[512,2048]{1,0:T(8,128)} %fusion.3, bf16[512,2048]{0,1:T(8,128)(2,1)} %all-gather.14.cloned.1.call-done, bf16[2048,2048]{0,1:T(8,128)(2,1)} %get-tuple-element.14), kind=kOutput, calls=%fused_computation.12 | convolution fusion | flops 4296015872 | bytes 18874368 | tf_op jit(solution)/shard_map/dot_general | solution.py:14
  400.5 34.0 %all-gather.8.cloned.1.call-done = bf16[512,2048]{0,1:T(8,128)(2,1)} async-done(((bf16[128,2048]{0,1:T(8,128)(2,1)}), bf16[512,2048]{0,1:T(8,128)(2,1)}) %all-gather.8.cloned.1.call-update) | async-done | bytes 2097168 | tf_op jit(solution)/shard_map/all_gather | solution.py:43
  434.5 10.5 %fusion.2 = f32[512,2048]{1,0:T(8,128)} fusion(bf16[512,2048]{0,1:T(8,128)(2,1)} %all-gather.8.cloned.1.call-done, bf16[2048,2048]{1,0:T(8,128)(2,1)} %bitcast_multiply_fusion.2), kind=kOutput, calls=%fused_computation.19 | convolution fusion | flops 4294967296 | bytes 14680064 | tf_op jit(solution)/shard_map/dot_general | solution.py:46
  445.1 8.3 %fusion = bf16[2048,2048]{0,1:T(8,128)(2,1)} fusion(bf16[512,2048]{0,1:T(8,128)(2,1)} %all-gather.12.cloned.1.call-done, bf16[512,2048]{1,0:T(8,128)(2,1)S(1)} %copy-done.4, bf16[2048,8]{0,1:T(8,128)(2,1)S(1)} %bitcast.51), kind=kOutput, calls=%fused_computation.4 | convolution fusion | flops 4307550208 | bytes 12615680 | tf_op jit(solution)/shard_map/dot_general | solution.py:20
  453.4 12.5 %copy.16 = bf16[2048,2048]{1,0:T(8,128)(2,1)} copy(bf16[2048,2048]{0,1:T(8,128)(2,1)} %fusion) | data formatting | bytes 16777216
  465.9 8.3 %fusion.1 = bf16[2048,2048]{0,1:T(8,128)(2,1)} fusion(bf16[512,2048]{0,1:T(8,128)(2,1)S(1)} %copy-done.1, bf16[512,2048]{1,0:T(8,128)(2,1)} %all-gather.6.cloned.1.call-done, bf16[2048,8]{0,1:T(8,128)(2,1)S(1)} %bitcast.52), kind=kOutput, calls=%fused_computation.5 | convolution fusion | flops 4307550208 | bytes 12615680 | tf_op jit(solution)/shard_map/dot_general | solution.py:20
  474.2 12.4 %copy.17 = bf16[2048,2048]{1,0:T(8,128)(2,1)} copy(bf16[2048,2048]{0,1:T(8,128)(2,1)} %fusion.1) | data formatting | bytes 16777216
  486.6 8.3 %multiply_convert_fusion = bf16[2048,2048]{1,0:T(8,128)(2,1)} fusion(bf16[512,2048]{0,1:T(8,128)(2,1)} %all-gather.8.cloned.1.call-done, bf16[512,2048]{1,0:T(8,128)(2,1)S(1)} %copy-done.3, bf16[2048,8]{0,1:T(8,128)(2,1)S(1)} %bitcast.49), kind=kOutput, calls=%fused_computation.6 | convolution fusion | flops 4307550208 | bytes 12615680 | tf_op jit(solution)/shard_map/dot_general | solution.py:20
  496.7 47.7 %reduce-scatter.7.cloned.1.call-done = f32[64,2048]{1,0:T(8,128)} async-done(((f32[512,2048]{1,0:T(8,128)}), f32[64,2048]{1,0:T(8,128)}) %reduce-scatter.7.cloned.1.call-update) | async-done | bytes 524304 | tf_op jit(solution)/shard_map/reduce_scatter | solution.py:45
  (38 shorter events, 8.7 us)
Async XLA Ops:
  7.2 31.9 %all-gather.10.cloned.1.call-start = ((), (), s32[]{:S(2)}) async-start(), calls=%async_computation.8 | async-start | bytes 2359296 | tf_op jit(solution)/shard_map/all_gather | solution.py:51
  7.9 80.5 %all-gather.6.cloned.1.call-start = ((), (), s32[]{:S(2)}) async-start(), calls=%async_computation.4 | async-start | bytes 2359296 | tf_op jit(solution)/shard_map/all_gather | solution.py:32
  8.7 138.2 %reduce-scatter.9.cloned.1.call-start = ((), (), s32[]{:S(2)}) async-start(), calls=%async_computation.9 | async-start | bytes 5242880 | tf_op jit(solution)/shard_map/reduce_scatter | solution.py:56
  49.5 0.7 copy-start.2
  49.6 244.7 %reduce-scatter.5.cloned.1.call-start = ((), (), s32[]{:S(2)}) async-start(), calls=%async_computation.5 | async-start | bytes 10485760 | tf_op jit(solution)/shard_map/reduce_scatter | solution.py:36
  88.4 7.9 %copy-start = (bf16[2048,2048]{0,1:T(8,128)(2,1)S(1)}, bf16[2048,2048]{0,1:T(8,128)(2,1)}, u32[]{:S(2)}) copy-start(bf16[2048,2048]{0,1:T(8,128)(2,1)} %get-tuple-element.13) | copy-start | bytes 25165828
  88.4 7.9 %copy-start.4 = (bf16[512,2048]{1,0:T(8,128)(2,1)S(1)}, bf16[512,2048]{1,0:T(8,128)(2,1)}, u32[]{:S(2)}) copy-start(bf16[512,2048]{1,0:T(8,128)(2,1)} %all-gather.6.cloned.1.call-done) | copy-start | bytes 6291460
  105.4 237.2 %all-gather.12.cloned.1.call-start = ((), (), s32[]{:S(2)}) async-start(), calls=%async_computation.10 | async-start | bytes 2621440 | tf_op jit(solution)/shard_map/all_gather | solution.py:64
  297.9 90.6 %all-gather.14.cloned.1.call-start = ((), (), s32[]{:S(2)}) async-start(), calls=%async_computation.11 | async-start | bytes 2621440 | tf_op jit(solution)/shard_map/all_gather | solution.py:65
  298.4 136.1 %all-gather.8.cloned.1.call-start = ((), (), s32[]{:S(2)}) async-start(), calls=%async_computation.6 | async-start | bytes 2621440 | tf_op jit(solution)/shard_map/all_gather | solution.py:43
  299.2 195.7 %reduce-scatter.11.cloned.1.call-start = ((), (), s32[]{:S(2)}) async-start(), calls=%async_computation.12 | async-start | bytes 4718592 | tf_op jit(solution)/shard_map/reduce_scatter | solution.py:70
  400.2 144.2 %reduce-scatter.7.cloned.1.call-start = ((), (), s32[]{:S(2)}) async-start(), calls=%async_computation.7 | async-start | bytes 4718592 | tf_op jit(solution)/shard_map/reduce_scatter | solution.py:45
  453.4 12.5 %copy-start.1 = (bf16[512,2048]{0,1:T(8,128)(2,1)S(1)}, bf16[512,2048]{0,1:T(8,128)(2,1)}, u32[]{:S(2)}) copy-start(bf16[512,2048]{0,1:T(8,128)(2,1)} %all-gather.14.cloned.1.call-done) | copy-start | bytes 6291460
  474.2 12.4 %copy-start.3 = (bf16[512,2048]{1,0:T(8,128)(2,1)S(1)}, bf16[512,2048]{1,0:T(8,128)(2,1)}, u32[]{:S(2)}) copy-start(bf16[512,2048]{1,0:T(8,128)(2,1)} %all-gather.10.cloned.1.call-done) | copy-start | bytes 6291460
Sparse Core Ops, SparseCore 0:
  9.9 29.1 all-gather.9
  40.9 27.7 all-gather.5
  71.0 75.8 reduce-scatter.8
  149.1 145.1 reduce-scatter.4
  298.0 44.5 all-gather.11
  344.0 44.4 all-gather.13
  390.0 44.4 all-gather.7
  437.9 51.9 reduce-scatter.10
  493.2 51.1 reduce-scatter.6
where the time goes:
time: 556 us; the launch traced here: 553 us
  waiting for transfers between devices  374 us (67%)
  matrix products  81 us (15%)
  local copies, waits for them, and re-layouts  50.1 us (9%)
  other arithmetic  32.8 us (6%)
  between operations  13.9 us (2%)
    reduce_scatter x1, waiting for transfers between devices, local(): lax.psum_scatter(jnp.concatenate([gate_part, up_part], axis=1), 'row', sc...  147 us
    unnamed x14, local copies, waits for them, and re-layouts  49.8 us
    reduce_scatter x1, waiting for transfers between devices, local(): lax.psum_scatter(jnp.dot(row_block, down_masked, preferred_element_type=j...  47.7 us
    all_gather x1, waiting for transfers between devices, local(): lax.all_gather(gate_grad, 'row', axis=0, tiled=True)  43.1 us
    reduce_scatter x1, waiting for transfers between devices, local(): lax.psum_scatter(transposed_right(row_block, down_masked), 'row', scatter...  41.5 us
    all_gather x1, waiting for transfers between devices, local(): lax.all_gather(up_grad, 'row', axis=0, tiled=True)  35.3 us
    all_gather x1, waiting for transfers between devices, local(): hidden_full = lax.all_gather(hidden_share, 'row', axis=0, tiled=True)  34 us
    dot_general x3, matrix products, transposed_right(): lax.dot_general(left, right, (((1,), (1,)), ((), ())), preferred_element_...  32.8 us
  transfers between devices with their start and end apart: 9, of which 7 were waited for; matrix products, arithmetic and copies ran while one was open for 29% of the time, Pallas kernels for 0%

commit v1 on v0

v1 whole, which is shorter than its diff:
```python
import functools

import jax
import jax.numpy as jnp
from jax import lax
from jax.experimental import pallas as pl
from jax.experimental.pallas import tpu as pltpu
from jax.sharding import PartitionSpec as P

BLOCK = 256
HALVES = 2
SLOTS = 4
LAG = 2
MESH = pl.DeviceIdType.MESH
F32 = jnp.float32
BF16 = jnp.bfloat16


def dot(left, right, dims):
    return lax.dot_general(left, right, (dims, ((), ())), preferred_element_type=F32)


def step_kernel(
    rows, cols, units,
    tok, cot, w_gate, w_up, w_down, keep_in, keep_out,
    out, tok_grad, x_out, dy_out, fin_out,
    x, dy, part, other, fin, own, w_in, w_dn, out_acc, tok_acc, rs_send, rs_recv,
    ag_ss, ag_rs, loc_s, w_s, p_ss, a_rs, b_rs, fi_ss, fo_ss, f_rs, x_s, fin_s, rs_ss, rs_rs,
):
    r = lax.axis_index("row")
    c = lax.axis_index("col")
    low = r < rows // 2
    inner = jnp.where(low, r + 1, r - 1)
    outer = jnp.where(low, r - 1, r + 1)
    has_outer = (r > 0) & (r < rows - 1)
    middle = (r == rows // 2 - 1) | (r == rows // 2)
    my_turn = jnp.where(low, 0, 1)
    share = tok.shape[0]
    width = x.shape[1]
    half = x.shape[0] // HALVES
    pieces = width // BLOCK

    def owns(k):
        return middle & (k % 2 == my_turn)

    def weights(k):
        s = k % SLOTS
        at = pl.ds(pl.multiple_of(k * BLOCK, BLOCK), BLOCK)
        return (
            pltpu.make_async_copy(w_gate.at[:, at], w_in.at[s, 0], w_s.at[s, 0]),
            pltpu.make_async_copy(w_up.at[:, at], w_in.at[s, 1], w_s.at[s, 1]),
            pltpu.make_async_copy(w_down.at[at, :], w_dn.at[s], w_s.at[s, 2]),
        )

    for copy in weights(0):
        copy.start()

    barrier = pltpu.get_barrier_semaphore()
    pl.semaphore_signal(barrier, inc=1, device_id=(inner, c), device_id_type=MESH)

    @pl.when(has_outer)
    def _():
        pl.semaphore_signal(barrier, inc=1, device_id=(outer, c), device_id_type=MESH)

    for i in range(1, cols):
        pl.semaphore_signal(
            barrier, inc=1, device_id=(r, lax.rem(c + i, cols)), device_id_type=MESH
        )
    pl.semaphore_wait(barrier, jnp.where(has_outer, cols + 1, cols))

    mine = pl.ds(pl.multiple_of(c * share, share), share)

    def gathers(j):
        src, dst = ((tok, x), (cot, dy))[j]
        return [
            pltpu.make_async_remote_copy(
                src_ref=src,
                dst_ref=dst.at[mine, :],
                send_sem=ag_ss.at[j, i - 1],
                recv_sem=ag_rs.at[j, i - 1],
                device_id=(r, lax.rem(c + i, cols)),
                device_id_type=MESH,
            )
            for i in range(1, cols)
        ]

    def own_copy(j):
        src, dst = ((tok, x), (cot, dy))[j]
        return pltpu.make_async_copy(src, dst.at[mine, :], loc_s.at[j])

    def saved(j):
        return pltpu.make_async_copy((x, dy)[j], (x_out, dy_out)[j], x_s.at[j])

    def gathered(j):
        own_copy(j).wait()
        for copy in gathers(j):
            copy.wait()
        saved(j).start()

    for j in range(2):
        own_copy(j).start()
        for copy in gathers(j):
            copy.start()

    out_acc[...] = jnp.zeros_like(out_acc)
    tok_acc[...] = jnp.zeros_like(tok_acc)
    gathered(0)

    def send_inner(k, h):
        return pltpu.make_async_remote_copy(
            src_ref=part.at[k, h], dst_ref=part.at[k, h], send_sem=p_ss.at[k, h],
            recv_sem=a_rs.at[k, h], device_id=(inner, c), device_id_type=MESH,
        )

    def send_middle(k, h):
        return pltpu.make_async_remote_copy(
            src_ref=part.at[k, h], dst_ref=other.at[k // 2, h], send_sem=p_ss.at[k, h],
            recv_sem=b_rs.at[k // 2, h], device_id=(inner, c), device_id_type=MESH,
        )

    def share_inner(k, h):
        return pltpu.make_async_remote_copy(
            src_ref=fin.at[k, h], dst_ref=fin.at[k, h], send_sem=fi_ss.at[k, h],
            recv_sem=f_rs.at[k, h], device_id=(inner, c), device_id_type=MESH,
        )

    def share_outer(k, h):
        return pltpu.make_async_remote_copy(
            src_ref=fin.at[k, h], dst_ref=fin.at[k, h], send_sem=fo_ss.at[k, h],
            recv_sem=f_rs.at[k, h], device_id=(outer, c), device_id_type=MESH,
        )

    def save_fin(k, h):
        return pltpu.make_async_copy(
            fin.at[k, h],
            fin_out.at[
                :,
                pl.ds(pl.multiple_of(h * half, half), half),
                pl.ds(pl.multiple_of(k * BLOCK, BLOCK), BLOCK),
            ],
            fin_s.at[k, h],
        )

    def produce(k):
        s = k % SLOTS
        for copy in weights(k):
            copy.wait()

        @pl.when(k + 1 < units)
        def _():
            for copy in weights(k + 1):
                copy.start()

        @pl.loop(0, pieces)
        def _(i):
            at = pl.ds(pl.multiple_of(i * BLOCK, BLOCK), BLOCK)
            keep = keep_in[k, i]
            w_in[s, 0, at, :] = (w_in[s, 0, at, :].astype(F32) * keep).astype(BF16)
            w_in[s, 1, at, :] = (w_in[s, 1, at, :].astype(F32) * keep).astype(BF16)
            w_dn[s, :, at] = (w_dn[s, :, at].astype(F32) * keep_out[k, i]).astype(BF16)

        @pl.loop(0, HALVES)
        def _(h):
            at = pl.ds(pl.multiple_of(h * half, half), half)
            own[k % 2, h, 0] = dot(x[at, :], w_in[s, 0], ((1,), (0,)))
            own[k % 2, h, 1] = dot(x[at, :], w_in[s, 1], ((1,), (0,)))

        @pl.when(k == 0)
        def _():
            gathered(1)

        @pl.loop(0, HALVES)
        def _(h):
            at = pl.ds(pl.multiple_of(h * half, half), half)
            own[k % 2, h, 2] = dot(dy[at, :], w_dn[s], ((1,), (1,)))

    def combine(k):
        b = k % 2

        @pl.loop(0, HALVES)
        def _(h):
            @pl.when(has_outer)
            def _():
                send_inner(k, h).wait_recv()
                for j in range(3):
                    own[b, h, j] += part[k, h, j].astype(F32)

            @pl.when(owns(k))
            def _():
                send_middle(k, h).wait_recv()
                gate = own[b, h, 0] + other[k // 2, h, 0].astype(F32)
                up = own[b, h, 1] + other[k // 2, h, 1].astype(F32)
                grad = own[b, h, 2] + other[k // 2, h, 2].astype(F32)
                sig = jax.nn.sigmoid(gate)
                act = gate * sig
                fin[k, h, 0] = (act * up).astype(BF16)
                fin[k, h, 1] = (grad * up * sig * (1.0 + gate * (1.0 - sig))).astype(BF16)
                fin[k, h, 2] = (grad * act).astype(BF16)
                share_inner(k, h).start()

            @pl.when(jnp.logical_not(owns(k)))
            def _():
                for j in range(3):
                    part[k, h, j] = own[b, h, j].astype(BF16)

                @pl.when(middle)
                def _():
                    send_middle(k, h).start()

                @pl.when(jnp.logical_not(middle))
                def _():
                    send_inner(k, h).start()

            @pl.when(owns(k) & has_outer)
            def _():
                share_outer(k, h).start()

    def consume(k):
        s = k % SLOTS

        @pl.loop(0, HALVES)
        def _(h):
            @pl.when(jnp.logical_not(owns(k)))
            def _():
                share_inner(k, h).wait_recv()

                @pl.when(has_outer)
                def _():
                    share_outer(k, h).start()

            save_fin(k, h).start()

        @pl.loop(0, HALVES)
        def _(h):
            at = pl.ds(pl.multiple_of(h * half, half), half)
            out_acc[at, :] += dot(fin[k, h, 0], w_dn[s], ((1,), (0,)))
            tok_acc[at, :] += dot(fin[k, h, 1], w_in[s, 0], ((1,), (1,))) + dot(
                fin[k, h, 2], w_in[s, 1], ((1,), (1,))
            )

    @pl.loop(0, units + LAG)
    def _(t):
        @pl.when(t < units)
        def _():
            produce(t)

        @pl.when((t >= 1) & (t <= units))
        def _():
            combine(t - 1)

        @pl.when(t >= LAG)
        def _():
            consume(t - LAG)

    def scatters(j):
        return [
            pltpu.make_async_remote_copy(
                src_ref=rs_send.at[
                    j, pl.ds(pl.multiple_of(lax.rem(c + i, cols) * share, share), share), :
                ],
                dst_ref=rs_recv.at[j, i - 1],
                send_sem=rs_ss.at[j, i - 1],
                recv_sem=rs_rs.at[j, i - 1],
                device_id=(r, lax.rem(c + i, cols)),
                device_id_type=MESH,
            )
            for i in range(1, cols)
        ]

    for j, acc in enumerate((out_acc, tok_acc)):
        rs_send[j] = acc[...].astype(BF16)
        for copy in scatters(j):
            copy.start()

    @pl.loop(0, units * HALVES)
    def _(n):
        k, h = n // HALVES, n % HALVES
        save_fin(k, h).wait()

        @pl.when(owns(k))
        def _():
            share_inner(k, h).wait_send()

        @pl.when(jnp.logical_not(owns(k)))
        def _():
            send_inner(k, h).wait_send()

        @pl.when(has_outer)
        def _():
            share_outer(k, h).wait_send()

    for j in range(2):
        saved(j).wait()

    for j, (acc, ref) in enumerate(((out_acc, out), (tok_acc, tok_grad))):
        for copy in scatters(j):
            copy.wait()
        total = acc[mine, :]
        for i in range(cols - 1):
            total = total + rs_recv[j, i].astype(F32)
        ref[...] = total.astype(BF16)


def wgrad_kernel(x, dy, fin, keep_in, keep_out, gate_w, up_w, down_w, x_t, h_t):
    k = pl.program_id(0)
    pieces = x.shape[1] // BLOCK

    @pl.when(k == 0)
    def _():
        @pl.loop(0, pieces)
        def _(i):
            at = pl.ds(pl.multiple_of(i * BLOCK, BLOCK), BLOCK)
            x_t[at, :] = x[:, at].T

    h_t[...] = fin[0].T

    @pl.loop(0, pieces)
    def _(i):
        at = pl.ds(pl.multiple_of(i * BLOCK, BLOCK), BLOCK)

        @pl.when(keep_in[k, i] != 0)
        def _():
            gate_w[at, :] = dot(x_t[at, :], fin[1], ((1,), (0,))).astype(BF16)
            up_w[at, :] = dot(x_t[at, :], fin[2], ((1,), (0,))).astype(BF16)

        @pl.when(keep_in[k, i] == 0)
        def _():
            gate_w[at, :] = jnp.zeros((BLOCK, BLOCK), BF16)
            up_w[at, :] = jnp.zeros((BLOCK, BLOCK), BF16)

        @pl.when(keep_out[k, i] != 0)
        def _():
            down_w[:, at] = dot(h_t[...], dy[:, at], ((1,), (0,))).astype(BF16)

        @pl.when(keep_out[k, i] == 0)
        def _():
            down_w[:, at] = jnp.zeros((BLOCK, BLOCK), BF16)


def local(rows, cols, tokens, w_gate, w_up, w_down, mask_in, mask_out, out_grad):
    share, width = tokens.shape
    hidden = w_gate.shape[1]
    units = hidden // BLOCK
    total = share * cols
    half = total // HALVES
    vmem = pl.BlockSpec(memory_space=pltpu.VMEM)
    smem = pl.BlockSpec(memory_space=pltpu.SMEM)
    anywhere = pl.BlockSpec(memory_space=pl.ANY)
    dma = pltpu.SemaphoreType.DMA
    sent = (units, HALVES)
    flops = 12 * total * width * hidden
    output, tokens_grad, x, dy, fin = pl.pallas_call(
        functools.partial(step_kernel, rows, cols, units),
        out_shape=(
            jax.ShapeDtypeStruct((share, width), BF16),
            jax.ShapeDtypeStruct((share, width), BF16),
            jax.ShapeDtypeStruct((total, width), BF16),
            jax.ShapeDtypeStruct((total, width), BF16),
            jax.ShapeDtypeStruct((3, total, hidden), BF16),
        ),
        in_specs=[vmem, vmem, anywhere, anywhere, anywhere, smem, smem],
        out_specs=(vmem, vmem, anywhere, anywhere, anywhere),
        scratch_shapes=[
            pltpu.VMEM((total, width), BF16),
            pltpu.VMEM((total, width), BF16),
            pltpu.VMEM((units, HALVES, 3, half, BLOCK), BF16),
            pltpu.VMEM(((units + 1) // 2, HALVES, 3, half, BLOCK), BF16),
            pltpu.VMEM((units, HALVES, 3, half, BLOCK), BF16),
            pltpu.VMEM((2, HALVES, 3, half, BLOCK), F32),
            pltpu.VMEM((SLOTS, 2, width, BLOCK), BF16),
            pltpu.VMEM((SLOTS, BLOCK, width), BF16),
            pltpu.VMEM((total, width), F32),
            pltpu.VMEM((total, width), F32),
            pltpu.VMEM((2, total, width), BF16),
            pltpu.VMEM((2, cols - 1, share, width), BF16),
            dma((2, cols - 1)),
            dma((2, cols - 1)),
            dma((2,)),
            dma((SLOTS, 3)),
            dma(sent),
            dma(sent),
            dma(((units + 1) // 2, HALVES)),
            dma(sent),
            dma(sent),
            dma(sent),
            dma((2,)),
            dma(sent),
            dma((2, cols - 1)),
            dma((2, cols - 1)),
        ],
        compiler_params=pltpu.CompilerParams(
            collective_id=0, has_side_effects=True, vmem_limit_bytes=63 * 1024 * 1024
        ),
        cost_estimate=pl.CostEstimate(
            flops=flops, bytes_accessed=6 * width * hidden, transcendentals=total * hidden
        ),
        name="step",
    )(
        tokens, out_grad, w_gate, w_up, w_down,
        mask_in.astype(F32), mask_out.astype(F32),
    )
    gate_wgrad, up_wgrad, down_wgrad = pl.pallas_call(
        wgrad_kernel,
        grid=(units,),
        out_shape=(
            jax.ShapeDtypeStruct((width, hidden), BF16),
            jax.ShapeDtypeStruct((width, hidden), BF16),
            jax.ShapeDtypeStruct((hidden, width), BF16),
        ),
        in_specs=[
            pl.BlockSpec((total, width), lambda k: (0, 0)),
            pl.BlockSpec((total, width), lambda k: (0, 0)),
            pl.BlockSpec((3, total, BLOCK), lambda k: (0, 0, k)),
            smem,
            smem,
        ],
        out_specs=(
            pl.BlockSpec((width, BLOCK), lambda k: (0, k)),
            pl.BlockSpec((width, BLOCK), lambda k: (0, k)),
            pl.BlockSpec((BLOCK, width), lambda k: (k, 0)),
        ),
        scratch_shapes=[pltpu.VMEM((width, total), BF16), pltpu.VMEM((BLOCK, total), BF16)],
        compiler_params=pltpu.CompilerParams(vmem_limit_bytes=40 * 1024 * 1024),
        name="wgrad",
    )(x, dy, fin, mask_in, mask_out)
    return output, tokens_grad, gate_wgrad, up_wgrad, down_wgrad


def solution(mesh):
    placed = (
        P("col", "row"),
        P("row", "col"),
        P("row", "col"),
        P("col", "row"),
        P("col", "row"),
        P("col", "row"),
        P("col", "row"),
    )
    return jax.shard_map(
        functools.partial(local, mesh.shape["row"], mesh.shape["col"]),
        mesh=mesh,
        in_specs=placed,
        out_specs=(
            P("col", "row"),
            P("col", "row"),
            P("row", "col"),
            P("row", "col"),
            P("col", "row"),
        ),
        check_vma=False,
    )
```

time: 556 us -> 529 us (0.951)
  Pallas kernels: 0 us -> 519 us
  waiting for transfers between devices: 374 us -> 0 us
  matrix products: 81 us -> 0 us
  local copies, waits for them, and re-layouts: 50.1 us -> 7.38 us
  other arithmetic: 32.8 us -> 2.56 us
  between operations: 13.9 us -> 0.67 us
    pallas_call x0 -> x2, Pallas kernels: none -> 519 us  [the longest x1 490 us: local(): pl.pallas_call(functools.partial(step_kernel, rows, cols, units), out_sha...]
    reduce_scatter x4 -> x0, waiting for transfers between devices: 237 us -> none  [the longest x1 147 us: local(): lax.psum_scatter(jnp.concatenate([gate_part, up_part], axis=1), 'row', sc...]
    all_gather x5 -> x0, waiting for transfers between devices: 135 us -> none  [the longest x1 43.1 us: local(): lax.all_gather(gate_grad, 'row', axis=0, tiled=True)]
    dot_general x9 -> x0, matrix products: 81 us -> none  [the longest x3 32.8 us: transposed_right(): lax.dot_general(left, right, (((1,), (1,)), ((), ())), preferred_element_...]
    unnamed x14 -> x16, local copies, waits for them, and re-layouts: 49.8 us -> 7.38 us
    mul x2 -> x0, other arithmetic: 20.8 us -> none  [the longest x1 13.5 us: local(): gate_masked = w_gate * keep_in]
  transfers between devices with their start and end apart: 9 -> 0, of which waited for: 7 -> 0; matrix products, arithmetic and copies ran while one was open for 29% -> 0% of each run, Pallas kernels for 0% -> 0%
where the time goes in v1:
time: 529 us
  Pallas kernels  519 us (98%)
  local copies, waits for them, and re-layouts  7.38 us (1%)
    pallas_call x1, Pallas kernels, local(): pl.pallas_call(functools.partial(step_kernel, rows, cols, units), out_sha...  490 us
    pallas_call x1, Pallas kernels, local(): pl.pallas_call(wgrad_kernel, grid=(units,), out_shape=(jax.ShapeDtypeStru...  28.6 us

profile of v1, /device:TPU:27, one launch (start us, length us, event | category | flops | bytes accessed | tf_op | source)
XLA Modules:
  0.0 529.5 jit_solution(10959099987272756032)
XLA Ops:
  0.6 1.3 convert_element_type.6.keep_in
  1.9 1.3 convert_element_type.7.keep_out
  3.2 0.0 copy-start.3
  3.2 0.0 copy-start.4
  3.2 490.2 %step.1 = (bf16[64,2048]{1,0:T(8,128)(2,1)}, bf16[64,2048]{1,0:T(8,128)(2,1)}, bf16[512,2048]{1,0:T(8,128)(2,1)}, bf16[512,2048]{1,0:T(8,128)(2,1)}, bf16[3,512,2048]{2,1,0:T(8,128)(2,1)}) custom-call(bf16[64,2048]{1,0:T(8,128)(2,1)} %tok.1, bf16[64,2048]{1,0:T(8,128)(2,1)} %cot.1, bf16[2048,2048]{1,0:T(8,128)(2,1)} %w_gate.1, bf16[2048,2048]{1,0:T(8,128)(2,1)} %w_up.1, ...), custom_call_target="tpu_custom_call" | custom-call | flops 25769803776 | bytes 25165824 | tf_op jit(solution)/shard_map/step/pallas_call | solution.py:352
  493.5 0.0 copy-done.3
  493.5 0.0 copy-done.4
  493.5 0.0 copy-start
  493.5 2.8 copy-done
  496.3 0.0 copy-start.1
  496.3 1.6 copy-done.1
  497.8 0.0 copy-start.2
  497.9 1.6 copy-done.2
  499.4 0.0 copy-start.6
  499.4 0.0 copy-start.5
  499.4 28.6 %wgrad.1 = (bf16[2048,2048]{1,0:T(8,128)(2,1)}, bf16[2048,2048]{1,0:T(8,128)(2,1)}, bf16[2048,2048]{1,0:T(8,128)(2,1)}) custom-call(bf16[512,2048]{1,0:T(8,128)(2,1)S(1)} %copy-done.1, bf16[512,2048]{1,0:T(8,128)(2,1)S(1)} %copy-done.2, bf16[3,512,2048]{2,1,0:T(8,128)(2,1)S(1)} %copy-done, s32[8,8]{1,0:T(8,128)S(1)} %copy-done.3, s32[8,8]{1,0:T(8,128)S(1)} %copy-done.4), custom_call_target="tpu_custom_call" | custom-call | tf_op jit(solution)/shard_map/wgrad/pallas_call | solution.py:402
  528.1 0.0 copy-done.6
  528.1 0.7 copy.14
  528.8 0.0 copy-done.5
  528.8 0.7 copy.15
Async XLA Ops:
  3.2 490.3 %copy-start.3 = (s32[8,8]{1,0:T(8,128)S(1)}, s32[8,8]{1,0:T(8,128)}, u32[]{:S(2)}) copy-start(s32[8,8]{1,0:T(8,128)} %keep_in.1) | copy-start | bytes 772
  3.2 490.3 %copy-start.4 = (s32[8,8]{1,0:T(8,128)S(1)}, s32[8,8]{1,0:T(8,128)}, u32[]{:S(2)}) copy-start(s32[8,8]{1,0:T(8,128)} %keep_out.1) | copy-start | bytes 772
  493.5 2.8 copy-start
  496.3 1.6 copy-start.1
  497.8 1.6 copy-start.2
  499.4 28.6 %copy-start.6 = (bf16[64,2048]{1,0:T(8,128)(2,1)S(1)}, bf16[64,2048]{1,0:T(8,128)(2,1)}, u32[]{:S(2)}) copy-start(bf16[64,2048]{1,0:T(8,128)(2,1)} %get-tuple-element.26) | copy-start | bytes 786436
  499.4 29.3 %copy-start.5 = (bf16[64,2048]{1,0:T(8,128)(2,1)S(1)}, bf16[64,2048]{1,0:T(8,128)(2,1)}, u32[]{:S(2)}) copy-start(bf16[64,2048]{1,0:T(8,128)(2,1)} %get-tuple-element.27) | copy-start | bytes 786436

commit v2 on v1

--- a/solution.py
+++ b/solution.py
@@ -9,8 +9,8 @@
 
 BLOCK = 256
 HALVES = 2
-SLOTS = 4
-LAG = 2
+SLOTS = 7
+LAG = 5
 MESH = pl.DeviceIdType.MESH
 F32 = jnp.float32
 BF16 = jnp.bfloat16

time: 529 us -> 402 us (0.76)
  Pallas kernels: 519 us -> 391 us
    pallas_call x1, Pallas kernels: 490 us -> 365 us  [local(): pl.pallas_call(functools.partial(step_kernel, rows, cols, units), out_sha...]
where the time goes in v2:
time: 402 us; the launch traced here: 401 us
  Pallas kernels  391 us (97%)
  local copies, waits for them, and re-layouts  7.38 us (2%)
    pallas_call x1, Pallas kernels, local(): pl.pallas_call(functools.partial(step_kernel, rows, cols, units), out_sha...  365 us
    pallas_call x1, Pallas kernels, local(): pl.pallas_call(wgrad_kernel, grid=(units,), out_shape=(jax.ShapeDtypeStru...  26 us

profile of v2, /device:TPU:27, one launch (start us, length us, event | category | flops | bytes accessed | tf_op | source)
XLA Modules:
  0.0 401.2 jit_solution(4480545328989763673)
XLA Ops:
  0.6 1.3 convert_element_type.6.keep_in
  1.9 1.3 convert_element_type.7.keep_out
  3.2 0.0 copy-start.3
  3.2 0.0 copy-start.4
  3.2 364.6 %step.1 = (bf16[64,2048]{1,0:T(8,128)(2,1)}, bf16[64,2048]{1,0:T(8,128)(2,1)}, bf16[512,2048]{1,0:T(8,128)(2,1)}, bf16[512,2048]{1,0:T(8,128)(2,1)}, bf16[3,512,2048]{2,1,0:T(8,128)(2,1)}) custom-call(bf16[64,2048]{1,0:T(8,128)(2,1)} %tok.1, bf16[64,2048]{1,0:T(8,128)(2,1)} %cot.1, bf16[2048,2048]{1,0:T(8,128)(2,1)} %w_gate.1, bf16[2048,2048]{1,0:T(8,128)(2,1)} %w_up.1, ...), custom_call_target="tpu_custom_call" | custom-call | flops 25769803776 | bytes 25165824 | tf_op jit(solution)/shard_map/step/pallas_call | solution.py:352
  367.8 0.0 copy-done.3
  367.8 0.0 copy-done.4
  367.8 0.0 copy-start
  367.8 2.8 copy-done
  370.6 0.0 copy-start.1
  370.6 1.6 copy-done.1
  372.2 0.0 copy-start.2
  372.2 1.6 copy-done.2
  373.8 0.0 copy-start.6
  373.8 0.0 copy-start.5
  373.8 26.0 %wgrad.1 = (bf16[2048,2048]{1,0:T(8,128)(2,1)}, bf16[2048,2048]{1,0:T(8,128)(2,1)}, bf16[2048,2048]{1,0:T(8,128)(2,1)}) custom-call(bf16[512,2048]{1,0:T(8,128)(2,1)S(1)} %copy-done.1, bf16[512,2048]{1,0:T(8,128)(2,1)S(1)} %copy-done.2, bf16[3,512,2048]{2,1,0:T(8,128)(2,1)S(1)} %copy-done, s32[8,8]{1,0:T(8,128)S(1)} %copy-done.3, s32[8,8]{1,0:T(8,128)S(1)} %copy-done.4), custom_call_target="tpu_custom_call" | custom-call | tf_op jit(solution)/shard_map/wgrad/pallas_call | solution.py:402
  399.8 0.0 copy-done.6
  399.8 0.7 copy.14
  400.5 0.0 copy-done.5
  400.5 0.7 copy.15
Async XLA Ops:
  3.2 364.6 %copy-start.3 = (s32[8,8]{1,0:T(8,128)S(1)}, s32[8,8]{1,0:T(8,128)}, u32[]{:S(2)}) copy-start(s32[8,8]{1,0:T(8,128)} %keep_in.1) | copy-start | bytes 772
  3.2 364.6 %copy-start.4 = (s32[8,8]{1,0:T(8,128)S(1)}, s32[8,8]{1,0:T(8,128)}, u32[]{:S(2)}) copy-start(s32[8,8]{1,0:T(8,128)} %keep_out.1) | copy-start | bytes 772
  367.8 2.8 copy-start
  370.6 1.6 copy-start.1
  372.2 1.6 copy-start.2
  373.8 26.0 %copy-start.6 = (bf16[64,2048]{1,0:T(8,128)(2,1)S(1)}, bf16[64,2048]{1,0:T(8,128)(2,1)}, u32[]{:S(2)}) copy-start(bf16[64,2048]{1,0:T(8,128)(2,1)} %get-tuple-element.26) | copy-start | bytes 786436
  373.8 26.7 %copy-start.5 = (bf16[64,2048]{1,0:T(8,128)(2,1)S(1)}, bf16[64,2048]{1,0:T(8,128)(2,1)}, u32[]{:S(2)}) copy-start(bf16[64,2048]{1,0:T(8,128)(2,1)} %get-tuple-element.27) | copy-start | bytes 786436
